TPU v7x, 32 devices: a whole 2x2x4 slice. The times are simulated.
32 devices in a mesh: groups: 2 (over x), pool: 8 (over z, y), shard: 2 (over core).
Axes of the slice: x: 2, y: 2, z: 4, core: 2. Of those that a mesh axis runs over, the one named last changes fastest.
Arguments:
- tokens: bfloat16 [2, 64, 8192], P(None, ('groups', 'pool'), 'shard'), parts along dimension 1, may hold values from -6 to 6
- counts: int32 [2, 16], P(None, ('groups', 'pool')), parts along dimension 1, may hold values from 0 to 4, as said below
- gate_up: bfloat16 [8192, 2, 28672], P('shard', None, 'pool'), may hold values from -0.0625 to 0.0625
- down: bfloat16 [28672, 8192], P('pool', 'shard'), may hold values from -0.03125 to 0.03125
Outputs:
- mixed: bfloat16 [2, 64, 8192], P(None, ('groups', 'pool'), 'shard'), parts along dimension 1
There are 2 independent parts, one for each index of `groups`. A program takes and returns all parts, laid end to end along the dimension named above; an argument that names none is the same for every part. Nothing has to cross between parts.
Inputs may be any that keep to these rules, and one draw needn't show every extreme that they name: `counts`: in each micro-batch some device has 4 live rows and some has none.
All inputs are finite; a program needn't handle non-finite values.
Results may differ from a plain program's by a relative error of at most 0.005.
Values may be sent and summed in bfloat16 or wider, within the bound.
A program may use at most 256 MiB of HBM per device.

v0:
```python
import jax
import jax.numpy as jnp
from jax import lax
from jax.sharding import PartitionSpec as P


def feed_forward(own_rows, gate_up, down):
    flat_weights = gate_up.reshape(gate_up.shape[0], -1)
    local_units = gate_up.shape[2]
    partial_sums = jnp.dot(
        lax.all_gather(own_rows, "pool", axis=0, tiled=True),
        flat_weights,
        preferred_element_type=jnp.float32,
    )
    row_total = partial_sums.shape[0]
    partial_sums = partial_sums.reshape(row_total, 2, local_units)
    summed = lax.psum(partial_sums, "shard")
    hidden = (jax.nn.silu(summed[:, 0]) * summed[:, 1]).astype(jnp.bfloat16)
    returned = lax.psum_scatter(
        jnp.dot(hidden, down, preferred_element_type=jnp.float32),
        "pool",
        scatter_dimension=0,
        tiled=True,
    )
    return returned.astype(jnp.bfloat16)


def shards(tokens, counts, gate_up, down):
    capacity = tokens.shape[1]
    position = lax.broadcasted_iota(jnp.int32, (capacity, 1), 0)
    nothing = jnp.zeros((), tokens.dtype)
    live_sets = [
        jnp.where(position < counts[micro_batch, 0], tokens[micro_batch], nothing)
        for micro_batch in range(tokens.shape[0])
    ]
    combined = jnp.concatenate(live_sets, axis=0)
    result = feed_forward(combined, gate_up, down)
    stacked = result.reshape(tokens.shape[0], capacity, result.shape[1])
    return stacked


def solution(mesh):
    placed = (
        P(None, ("groups", "pool"), "shard"),
        P(None, ("groups", "pool")),
        P("shard", None, "pool"),
        P("pool", "shard"),
    )
    return jax.shard_map(
        shards,
        mesh=mesh,
        in_specs=placed,
        out_specs=P(None, ("groups", "pool"), "shard"),
        check_vma=False,
    )
```

profile of v0, /device:TPU:0, one launch (start us, length us, event | category | flops | bytes accessed | tf_op | source)
XLA Modules:
  0.0 288.1 jit_solution(295380920429154931)
XLA Ops:
  6.5 0.0 all-reduce.2.cloned.1.call-start
  6.5 39.3 %copy.6 = bf16[512,8,2,3584]{3,1,2,0:T(8,128)(2,1)} copy(bf16[512,8,2,3584]{3,2,1,0:T(2,128)(2,1)} %bitcast.30) | data formatting | bytes 117440512
  45.8 0.0 copy-start.1
  45.8 0.0 copy-start
  45.8 69.5 %copy.5 = bf16[7168,4096]{1,0:T(8,128)(2,1)} copy(bf16[7168,4096]{0,1:T(8,128)(2,1)} %bitcast.29) | data formatting | bytes 117440512 | tf_op jit(solution)/shard_map/dot_general | solution.py:10
  115.3 0.0 copy-done.1
  115.3 0.6 fusion.8
  115.9 1.3 iota_compare_fusion
  117.3 0.0 copy-done
  117.3 0.1 bitcast_select_fusion.1
  117.4 33.0 %all_gather.3 = bf16[64,4096]{1,0:T(8,128)(2,1)S(1)} all-gather(bf16[8,4096]{1,0:T(8,128)(2,1)S(1)} %pad_maximum_fusion), channel_id=1, replica_groups=mesh['groups'=2,'pool'=8,'shard'=2] {'pool'}, dimensions={0}, use_global_device_ids=true | all-gather | bytes 589824 | tf_op jit(solution)/shard_map/all_gather | solution.py:11
  150.5 25.4 %fusion.2 = f32[64,2,3584]{2,0,1:T(8,128)} fusion(bf16[2,3584,4096]{2,1,0:T(8,128)(2,1)} %bitcast.28, bf16[64,4096]{1,0:T(8,128)(2,1)S(1)} %all_gather.3), kind=kOutput, calls=%fused_computation.4 | convolution fusion | flops 3758096384 | bytes 61079552 | tf_op jit(solution)/shard_map/dot_general | solution.py:10
  175.9 0.0 all-reduce.2.cloned.1.call-update
  175.9 0.0 reduce-scatter.2.cloned.1.call-start
  176.0 22.0 %all-reduce.2.cloned.1.call-done = f32[64,2,3584]{2,0,1:T(8,128)} async-done(((f32[64,2,3584]{2,0,1:T(8,128)}), f32[64,2,3584]{2,0,1:T(8,128)}) %all-reduce.2.cloned.1.call-update) | async-done | bytes 1835024 | tf_op jit(solution)/shard_map/psum | solution.py:17
  198.0 16.1 %fusion.4 = f32[64,4096]{1,0:T(8,128)} fusion(bf16[3584,4096]{1,0:T(8,128)(2,1)} %param.7, f32[64,2,3584]{2,0,1:T(8,128)} %all-reduce.2.cloned.1.call-done), kind=kOutput, calls=%fused_computation.6 | convolution fusion | flops 1880424448 | bytes 32243712 | tf_op jit(solution)/shard_map/dot_general | solution.py:20
  214.1 0.0 reduce-scatter.2.cloned.1.call-update
  214.1 65.6 %reduce-scatter.2.cloned.1.call-done = f32[8,4096]{1,0:T(8,128)} async-done(((f32[64,4096]{1,0:T(8,128)}), f32[8,4096]{1,0:T(8,128)}) %reduce-scatter.2.cloned.1.call-update) | async-done | bytes 131088 | tf_op jit(solution)/shard_map/reduce_scatter | solution.py:19
  279.7 0.9 convert_element_type.7
  280.6 0.7 reshape.19
  (1 shorter events, 0.0 us)
Async XLA Ops:
  6.5 191.5 %all-reduce.2.cloned.1.call-start = ((), (), s32[]{:S(2)}) async-start(), calls=%async_computation.1 | async-start | bytes 3670016 | tf_op jit(solution)/shard_map/psum | solution.py:17
  45.8 69.5 %copy-start.1 = (s32[2,1]{0,1:T(1,128)S(1)}, s32[2,1]{0,1:T(1,128)}, u32[]{:S(2)}) copy-start(s32[2,1]{0,1:T(1,128)} %param.5) | copy-start | bytes 28
  45.8 71.5 %copy-start = (bf16[2,4,4096]{2,1,0:T(4,128)(2,1)S(1)}, bf16[2,4,4096]{2,1,0:T(4,128)(2,1)}, u32[]{:S(2)}) copy-start(bf16[2,4,4096]{2,1,0:T(4,128)(2,1)} %param.4) | copy-start | bytes 196612
  175.9 103.8 %reduce-scatter.2.cloned.1.call-start = ((), (), s32[]{:S(2)}) async-start(), calls=%async_computation.2 | async-start | bytes 1179648 | tf_op jit(solution)/shard_map/reduce_scatter | solution.py:19
Sparse Core Ops, SparseCore 0:
  176.0 21.9 all-reduce.1
  214.3 65.3 reduce-scatter.1
where the time goes:
time: 290 us; the launch traced here: 288 us
  local copies, waits for them, and re-layouts  110 us (38%)
  waiting for transfers between devices  87.6 us (30%)
  matrix products  41.5 us (14%)
  blocking collectives  33 us (11%)
  between operations  13.4 us (5%)
    dot_general x1, local copies, waits for them, and re-layouts, feed_forward(): jnp.dot(lax.all_gather(own_rows, 'pool', axis=0, tiled=True), flat_weight...  69.5 us
    reduce_scatter x1, waiting for transfers between devices, feed_forward(): lax.psum_scatter(jnp.dot(hidden, down, preferred_element_type=jnp.float32...  65.6 us
    unnamed x5, local copies, waits for them, and re-layouts  39.3 us
    all_gather x1, blocking collectives, feed_forward(): lax.all_gather(own_rows, 'pool', axis=0, tiled=True)  33 us
    dot_general x1, matrix products, feed_forward(): jnp.dot(lax.all_gather(own_rows, 'pool', axis=0, tiled=True), flat_weight...  25.4 us
    psum x1, waiting for transfers between devices, feed_forward(): summed = lax.psum(partial_sums, 'shard')  22 us
    dot_general x1, matrix products, feed_forward(): jnp.dot(hidden, down, preferred_element_type=jnp.float32)  16.1 us
  transfers between devices with their start and end apart: 2, of which 2 were waited for; matrix products, arithmetic and copies ran while one was open for 0% of the time, Pallas kernels for 0%

commit v1 on v0

--- a/solution.py
+++ b/solution.py
@@ -14,7 +14,7 @@
     )
     row_total = partial_sums.shape[0]
     partial_sums = partial_sums.reshape(row_total, 2, local_units)
-    summed = lax.psum(partial_sums, "shard")
+    summed = jnp.sum(lax.all_gather(partial_sums, "shard"), axis=0)
     hidden = (jax.nn.silu(summed[:, 0]) * summed[:, 1]).astype(jnp.bfloat16)
     returned = lax.psum_scatter(
         jnp.dot(hidden, down, preferred_element_type=jnp.float32),

time: 290 us -> 282 us (0.972)
  waiting for transfers between devices: 87.6 us -> 79.8 us
  matrix products: 41.5 us -> 38.4 us
    psum x1 -> x0, waiting for transfers between devices: 22 us -> none  [feed_forward(): summed = lax.psum(partial_sums, 'shard')]
    all_gather x0 -> x1, waiting for transfers between devices: none -> 14.1 us  [feed_forward(): summed = jnp.sum(lax.all_gather(partial_sums, 'shard'), axis=0)]
    dot_general x1, matrix products: 16.1 us -> 13 us  [feed_forward(): jnp.dot(hidden, down, preferred_element_type=jnp.float32)]
where the time goes in v1:
time: 282 us; the launch traced here: 280 us
  local copies, waits for them, and re-layouts  110 us (39%)
  waiting for transfers between devices  79.8 us (28%)
  matrix products  38.4 us (14%)
  blocking collectives  33 us (12%)
  between operations  13.4 us (5%)
  other arithmetic  4.84 us (2%)
    dot_general x1, local copies, waits for them, and re-layouts, feed_forward(): jnp.dot(lax.all_gather(own_rows, 'pool', axis=0, tiled=True), flat_weight...  69.5 us
    reduce_scatter x1, waiting for transfers between devices, feed_forward(): lax.psum_scatter(jnp.dot(hidden, down, preferred_element_type=jnp.float32...  65.6 us
    unnamed x5, local copies, waits for them, and re-layouts  39.3 us
    all_gather x1, blocking collectives, feed_forward(): lax.all_gather(own_rows, 'pool', axis=0, tiled=True)  33 us
    dot_general x1, matrix products, feed_forward(): jnp.dot(lax.all_gather(own_rows, 'pool', axis=0, tiled=True), flat_weight...  25.4 us
    all_gather x1, waiting for transfers between devices, feed_forward(): summed = jnp.sum(lax.all_gather(partial_sums, 'shard'), axis=0)  14.1 us
    dot_general x1, matrix products, feed_forward(): jnp.dot(hidden, down, preferred_element_type=jnp.float32)  13 us
  transfers between devices with their start and end apart: 2, of which 2 were waited for; matrix products, arithmetic and copies ran while one was open for 0% of the time, Pallas kernels for 0%

profile of v1, /device:TPU:0, one launch (start us, length us, event | category | flops | bytes accessed | tf_op | source)
XLA Modules:
  0.0 279.6 jit_solution(17432752071016515698)
XLA Ops:
  6.5 0.0 all-gather.3.cloned.1.call-start
  6.5 39.3 %copy.8 = bf16[512,8,2,3584]{3,1,2,0:T(8,128)(2,1)} copy(bf16[512,8,2,3584]{3,2,1,0:T(2,128)(2,1)} %bitcast.31) | data formatting | bytes 117440512
  45.8 0.0 copy-start.1
  45.8 0.0 copy-start
  45.8 69.5 %copy.7 = bf16[7168,4096]{1,0:T(8,128)(2,1)} copy(bf16[7168,4096]{0,1:T(8,128)(2,1)} %bitcast.30) | data formatting | bytes 117440512 | tf_op jit(solution)/shard_map/dot_general | solution.py:10
  115.3 0.0 copy-done.1
  115.3 0.6 fusion.8
  115.9 1.3 iota_compare_fusion
  117.3 0.0 copy-done
  117.3 0.1 bitcast_select_fusion.1
  117.4 33.0 %all_gather.6 = bf16[64,4096]{1,0:T(8,128)(2,1)S(1)} all-gather(bf16[8,4096]{1,0:T(8,128)(2,1)S(1)} %pad_maximum_fusion), channel_id=1, replica_groups=mesh['groups'=2,'pool'=8,'shard'=2] {'pool'}, dimensions={0}, use_global_device_ids=true | all-gather | bytes 589824 | tf_op jit(solution)/shard_map/all_gather | solution.py:11
  150.5 25.4 %fusion.2 = f32[64,2,3584]{2,0,1:T(8,128)} fusion(bf16[2,3584,4096]{2,1,0:T(8,128)(2,1)} %bitcast.29, bf16[64,4096]{1,0:T(8,128)(2,1)S(1)} %all_gather.6), kind=kOutput, calls=%fused_computation.4 | convolution fusion | flops 3758096384 | bytes 61079552 | tf_op jit(solution)/shard_map/dot_general | solution.py:10
  175.9 0.0 all-gather.3.cloned.1.call-update
  175.9 0.0 reduce-scatter.2.cloned.1.call-start
  176.0 14.1 %all-gather.3.cloned.1.call-done = f32[128,2,3584]{2,0,1:T(8,128)} async-done(((f32[64,2,3584]{2,0,1:T(8,128)}), f32[128,2,3584]{2,0,1:T(8,128)}) %all-gather.3.cloned.1.call-update) | async-done | bytes 3670032 | tf_op jit(solution)/shard_map/all_gather | solution.py:17
  190.1 2.5 reduce_sum.9
  192.5 13.0 %fusion.4 = f32[64,4096]{1,0:T(8,128)} fusion(bf16[3584,4096]{1,0:T(8,128)(2,1)} %param.7, f32[64,2,3584]{2,0,1:T(8,128)S(1)} %reduce_sum.9), kind=kOutput, calls=%fused_computation.6 | convolution fusion | flops 1880424448 | bytes 32243712 | tf_op jit(solution)/shard_map/dot_general | solution.py:20
  205.6 0.0 reduce-scatter.2.cloned.1.call-update
  205.6 65.6 %reduce-scatter.2.cloned.1.call-done = f32[8,4096]{1,0:T(8,128)} async-done(((f32[64,4096]{1,0:T(8,128)}), f32[8,4096]{1,0:T(8,128)}) %reduce-scatter.2.cloned.1.call-update) | async-done | bytes 131088 | tf_op jit(solution)/shard_map/reduce_scatter | solution.py:19
  271.2 0.9 convert_element_type.7
  272.1 0.7 reshape.22
  (1 shorter events, 0.0 us)
Async XLA Ops:
  6.5 183.5 %all-gather.3.cloned.1.call-start = ((), (), s32[]{:S(2)}) async-start(), calls=%async_computation.2 | async-start | bytes 5505024 | tf_op jit(solution)/shard_map/all_gather | solution.py:17
  45.8 69.5 %copy-start.1 = (s32[2,1]{0,1:T(1,128)S(1)}, s32[2,1]{0,1:T(1,128)}, u32[]{:S(2)}) copy-start(s32[2,1]{0,1:T(1,128)} %param.5) | copy-start | bytes 28
  45.8 71.5 %copy-start = (bf16[2,4,4096]{2,1,0:T(4,128)(2,1)S(1)}, bf16[2,4,4096]{2,1,0:T(4,128)(2,1)}, u32[]{:S(2)}) copy-start(bf16[2,4,4096]{2,1,0:T(4,128)(2,1)} %param.4) | copy-start | bytes 196612
  175.9 95.3 %reduce-scatter.2.cloned.1.call-start = ((), (), s32[]{:S(2)}) async-start(), calls=%async_computation.1 | async-start | bytes 1179648 | tf_op jit(solution)/shard_map/reduce_scatter | solution.py:19
Sparse Core Ops, SparseCore 0:
  176.0 13.9 all-gather.2
  205.7 65.4 reduce-scatter.1
